TPU v7x, 128 devices: a whole 4x4x4 slice. The times are simulated.
128 devices in a mesh: ent: 32 (over x_hi, z, y), sec: 4 (over x_lo, core).
Axes of the slice: x: 4 (x_hi: 2, x_lo: 2; x = x_hi * 2 + x_lo), y: 4, z: 4, core: 2. Of those that a mesh axis runs over, the one named last changes fastest.
Arguments:
- features: bfloat16 [4096, 256], P('ent'), may hold values from -6 to 6
- theta: bfloat16 [256, 256], replicated, may hold values from -3 to 3
- section_weight: float32 [65536], P(('ent', 'sec')), may hold values from 0.5 to 2
- pair_rows: int32 [128, 32, 512], P(('ent', 'sec')), may hold values from 0 to 511
- pair_cols: int32 [128, 32, 512], P(('ent', 'sec')), may hold values from 0 to 127
- pair_counts: int32 [128, 32], P(('ent', 'sec')), may hold values from 0 to 512, as said below
- cotangent: bfloat16 [4096, 256], P('ent'), may hold values from -24 to 24
Outputs:
- activated: bfloat16 [4096, 256], P('ent')
- grad_features: bfloat16 [4096, 256], P('ent')
- grad_theta: float32 [256, 256], replicated
- grad_weight: float32 [65536], P(('ent', 'sec'))
Inputs may be any that keep to these rules, and one draw needn't show every extreme that they name: Only the first pair_counts[k, j] slots of shard k and block j are used; some shard uses all 512 slots of some block.
All inputs are finite; a program needn't handle non-finite values.
Results may differ from a plain program's by a relative error of at most 0.0059.
Values may be sent and summed in bfloat16 or wider, within the bound.
A program may use at most 64 MiB of HBM per device.

v0:
```python
import jax
import jax.numpy as jnp
from jax import lax
from jax.sharding import PartitionSpec as P


def hot_table(indices, live_slots, offset, table_width):
    hits = (indices - offset)[:, None] == jnp.arange(table_width, dtype=jnp.int32)[None, :]
    return (hits & live_slots[:, None]).astype(jnp.bfloat16)


def body(features, theta, section_weight, pair_rows, pair_cols, pair_counts, cotangent):
    ent_dev = features.shape[0]
    feature_width = features.shape[1]
    sec_dev = section_weight.shape[0]
    blocks_count = pair_rows.shape[1]
    slot_count = pair_rows.shape[2]
    own_block = lax.axis_index("ent")
    row_lists = pair_rows[0]
    col_lists = pair_cols[0]
    usable = jnp.arange(slot_count, dtype=jnp.int32)[None, :] < pair_counts[0][:, None]
    usable_float = usable.astype(jnp.float32)
    entity_index = jnp.arange(blocks_count, dtype=jnp.int32)[:, None] * ent_dev + col_lists
    local_degree = jax.ops.segment_sum(
        usable_float.reshape(-1), entity_index.reshape(-1), num_segments=blocks_count * ent_dev
    )
    entity_degree = lax.psum(local_degree, ("ent", "sec"))
    own_degree = lax.dynamic_slice_in_dim(entity_degree, own_block * ent_dev, ent_dev)
    entity_scale = lax.rsqrt(1.0 + own_degree)[:, None]
    sec_count = jax.ops.segment_sum(
        usable_float.reshape(-1), row_lists.reshape(-1), num_segments=sec_dev
    )
    section_scale = (section_weight / (1.0 + sec_count))[:, None]

    def entity_fold(running, incoming, start_row):
        row_count = incoming.shape[0]
        span_width = min(row_count, ent_dev)
        block_span = max(row_count // ent_dev, 1)
        offset = start_row

        def add_block(turn_index, accum):
            row_slots = lax.dynamic_index_in_dim(row_lists, turn_index, 0, keepdims=False)
            col_slots = lax.dynamic_index_in_dim(col_lists, turn_index, 0, keepdims=False)
            live_slots = lax.dynamic_index_in_dim(usable, turn_index, 0, keepdims=False)
            values = lax.dynamic_slice_in_dim(incoming, turn_index * span_width, span_width, 0)
            col_hot = hot_table(col_slots, live_slots, offset, span_width)
            row_hot = hot_table(row_slots, live_slots, 0, sec_dev)
            picked = jnp.dot(col_hot, values, preferred_element_type=jnp.float32).astype(
                jnp.bfloat16
            )
            return accum + jnp.einsum(
                "ps,pf->sf", row_hot, picked, preferred_element_type=jnp.float32
            )

        return lax.fori_loop(0, block_span, add_block, running)

    def entity_terms(messages, start_row):
        span_width = min(lax.axis_size("ent") * ent_dev, ent_dev)
        block_span = max(lax.axis_size("ent") * ent_dev // ent_dev, 1)
        offset = start_row

        def block_term(turn_index):
            row_slots = lax.dynamic_index_in_dim(row_lists, turn_index, 0, keepdims=False)
            col_slots = lax.dynamic_index_in_dim(col_lists, turn_index, 0, keepdims=False)
            live_slots = lax.dynamic_index_in_dim(usable, turn_index, 0, keepdims=False)
            row_hot = hot_table(row_slots, live_slots, 0, sec_dev)
            col_hot = hot_table(col_slots, live_slots, offset, span_width)
            picked = jnp.dot(row_hot, messages, preferred_element_type=jnp.float32).astype(
                jnp.bfloat16
            )
            return jnp.einsum("pw,pf->wf", col_hot, picked, preferred_element_type=jnp.float32)

        pieces = lax.map(block_term, jnp.arange(block_span, dtype=jnp.int32))
        return pieces.reshape(block_span * span_width, feature_width)

    def collect(messages):
        partial_sum = lax.psum_scatter(
            entity_terms(messages, jnp.int32(0)), "ent", scatter_dimension=0, tiled=True
        )
        return lax.psum(partial_sum, "sec")

    zero_sections = jnp.zeros((sec_dev, feature_width), jnp.float32)
    projected = jnp.dot(features, theta, preferred_element_type=jnp.float32)
    scaled = (entity_scale * projected).astype(jnp.bfloat16)
    gathered = entity_fold(
        zero_sections, lax.all_gather(scaled, "ent", axis=0, tiled=True), jnp.int32(0)
    )
    messages = (section_scale * gathered).astype(jnp.bfloat16)
    collected = collect(messages)
    preact = entity_scale * collected
    activated = jax.nn.silu(preact).astype(jnp.bfloat16)
    sigmoid_pre = jax.nn.sigmoid(preact)
    grad_pre = cotangent.astype(jnp.float32) * sigmoid_pre * (1.0 + preact * (1.0 - sigmoid_pre))
    back_scaled = (entity_scale * grad_pre).astype(jnp.bfloat16)
    back_gathered = entity_fold(
        zero_sections, lax.all_gather(back_scaled, "ent", axis=0, tiled=True), jnp.int32(0)
    )
    grad_weight = jnp.sum(gathered * back_gathered, axis=1) / (1.0 + sec_count)
    back_messages = (section_scale * back_gathered).astype(jnp.bfloat16)
    back_collected = collect(back_messages)
    grad_proj = (entity_scale * back_collected).astype(jnp.bfloat16)
    grad_features = lax.dot_general(
        grad_proj, theta, (((1,), (1,)), ((), ())), preferred_element_type=jnp.float32
    ).astype(jnp.bfloat16)
    local_theta = lax.dot_general(
        features, grad_proj, (((0,), (0,)), ((), ())), preferred_element_type=jnp.float32
    )
    grad_theta = lax.psum(local_theta, "ent")
    return (activated, grad_features, grad_theta, grad_weight)


def solution(mesh):
    placed = (
        P("ent", None),
        P(),
        P(("ent", "sec")),
        P(("ent", "sec"), None, None),
        P(("ent", "sec"), None, None),
        P(("ent", "sec"), None),
        P("ent", None),
    )
    return jax.shard_map(
        body,
        mesh=mesh,
        in_specs=placed,
        out_specs=(P("ent", None), P("ent", None), P(), P(("ent", "sec"))),
        check_vma=False,
    )
```

profile of v0, /device:TPU:0, one launch (start us, length us, event | category | flops | bytes accessed | tf_op | source)
XLA Modules:
  0.0 1644.0 jit_solution(5554662827985014451)
XLA Ops:
  9.2 113.5 %scatter_custom_fusion = f32[4096]{0:T(1024)S(1)} fusion(s32[16384]{0:T(1024)S(1)} %bitcast.81, f32[16384]{0:T(1024)S(1)} %bitcast.82, f32[]{:T(128)} %constant.131.clone.1), kind=kCustom, calls=%fused_computation.76 | custom fusion | flops 16384 | bytes 16388 | tf_op jit(solution)/shard_map/scatter-add | solution.py:24
  122.6 68.3 %psum.28 = f32[4096]{0:T(1024)S(1)} all-reduce(f32[4096]{0:T(1024)S(1)} %scatter_custom_fusion), channel_id=1, replica_groups=mesh['ent'=32,'sec'=4] {'ent','sec'}, use_global_device_ids=true, to_apply=%region_1.0 | all-reduce | flops 4096 | bytes 32768 | tf_op jit(solution)/shard_map/psum | solution.py:27
  193.5 113.4 %scatter_custom_fusion.1 = f32[512]{0:T(512)S(1)} fusion(s32[16384]{0:T(1024)S(1)} %bitcast.84, f32[16384]{0:T(1024)S(1)} %bitcast.83, f32[]{:T(128)} %constant.137.clone.1), kind=kCustom, calls=%fused_computation.78 | custom fusion | flops 16384 | bytes 2052 | tf_op jit(solution)/shard_map/scatter-add | solution.py:30
  307.7 79.9 %while.50 = (s32[]{:T(128)}, f32[512,256]{1,0:T(8,128)S(1)}, s32[32,512]{1,0:T(8,128)}, pred[32,512]{1,0:T(8,128)(4,1)S(1)}, s32[32,512]{1,0:T(8,128)}, /*index=...) while((s32[]{:T(128)}, f32[512,256]{1,0:T(8,128)S(1)}, ...), condition=%wide.region_4.5_spmd.clone, body=%wide.region_3.4_spmd.clone.sunk | while | flops 168820736 | bytes 1128617 | solution.py:55
  313.4 1.7 convolution_add_fusion.4
  315.9 1.7 convolution_add_fusion.4
  330.9 1.7 convolution_add_fusion.4
  333.4 1.7 convolution_add_fusion.4
  348.4 1.7 convolution_add_fusion.4
  350.9 1.7 convolution_add_fusion.4
  365.9 1.7 convolution_add_fusion.4
  368.4 1.7 convolution_add_fusion.4
  383.4 1.7 convolution_add_fusion.4
  385.9 1.7 convolution_add_fusion.4
  387.7 2.4 broadcast.21.clone
  390.2 144.5 %while.48 = (s32[]{:T(128)}, f32[32,128,256]{2,1,0:T(8,128)}, s32[32]{0:T(128)S(1)}, s32[32,512]{1,0:T(8,128)}, pred[32,512]{1,0:T(8,128)(4,1)S(1)}, /*index=5*/...) while((s32[]{:T(128)}, f32[32,128,256]{2,1,0:T(8,128)}, ...), condition=%wide.region_6.7_spmd, body=%wide.region_5.6_spmd.sunk | while | flops 168558592 | bytes 408219 | solution.py:73
  534.8 188.6 %reduce-scatter.3.cloned.1.call-done = f32[128,256]{1,0:T(8,128)} async-done(((f32[4096,256]{1,0:T(8,128)}), f32[128,256]{1,0:T(8,128)}) %reduce-scatter.3.cloned.1.call-update) | async-done | bytes 131088 | tf_op jit(solution)/shard_map/reduce_scatter | solution.py:77
  723.4 32.8 %all-reduce.4.cloned.1.call-done = f32[128,256]{1,0:T(8,128)} async-done(((f32[128,256]{1,0:T(8,128)}), f32[128,256]{1,0:T(8,128)}) %all-reduce.4.cloned.1.call-update) | async-done | bytes 131088 | tf_op jit(solution)/shard_map/psum | solution.py:80
  756.2 1.7 multiply_convert_fusion.3
  758.0 73.9 %all-gather.5.cloned.1.call-done = bf16[4096,256]{1,0:T(8,128)(2,1)} async-done(((bf16[128,256]{1,0:T(8,128)(2,1)}), bf16[4096,256]{1,0:T(8,128)(2,1)}) %all-gather.5.cloned.1.call-update) | async-done | bytes 2097168 | tf_op jit(solution)/shard_map/all_gather | solution.py:96
  831.9 79.9 %while.51 = (s32[]{:T(128)}, f32[512,256]{1,0:T(8,128)S(1)}, s32[32,512]{1,0:T(8,128)}, pred[32,512]{1,0:T(8,128)(4,1)S(1)}, s32[32,512]{1,0:T(8,128)}, /*index=...) while((s32[]{:T(128)}, f32[512,256]{1,0:T(8,128)S(1)}, ...), condition=%wide.region_10.11_spmd.clone, body=%wide.region_9.10_spmd.clone.sunk | while | flops 168820736 | bytes 1128617 | solution.py:55
  832.6 1.7 convolution_add_fusion.5
  842.6 1.7 convolution_add_fusion.5
  845.1 1.7 convolution_add_fusion.5
  912.0 2.4 broadcast.21
  914.4 144.5 %while.49 = (s32[]{:T(128)}, f32[32,128,256]{2,1,0:T(8,128)}, s32[32]{0:T(128)S(1)}, s32[32,512]{1,0:T(8,128)}, pred[32,512]{1,0:T(8,128)(4,1)S(1)}, /*index=5*/...) while((s32[]{:T(128)}, f32[32,128,256]{2,1,0:T(8,128)}, ...), condition=%wide.region_12.13_spmd, body=%wide.region_11.12_spmd.sunk | while | flops 168558592 | bytes 408219 | solution.py:73
  1059.0 190.6 %reduce-scatter.5.cloned.1.call-done = f32[128,256]{1,0:T(8,128)} async-done(((f32[4096,256]{1,0:T(8,128)}), f32[128,256]{1,0:T(8,128)}) %reduce-scatter.5.cloned.1.call-update) | async-done | bytes 131088 | tf_op jit(solution)/shard_map/reduce_scatter | solution.py:77
  1249.7 32.8 %all-reduce.6.cloned.1.call-done = f32[128,256]{1,0:T(8,128)} async-done(((f32[128,256]{1,0:T(8,128)}), f32[128,256]{1,0:T(8,128)}) %all-reduce.6.cloned.1.call-update) | async-done | bytes 131088 | tf_op jit(solution)/shard_map/psum | solution.py:80
  1282.5 1.9 convolution_bitcast_fusion
  1285.0 1.7 convolution_convert_fusion.4
  1286.8 348.6 %all-reduce.8.cloned.1.call-done = f32[256,256]{0,1:T(8,128)} async-done(((f32[256,256]{0,1:T(8,128)}), f32[256,256]{0,1:T(8,128)}) %all-reduce.8.cloned.1.call-update) | async-done | bytes 262160 | tf_op jit(solution)/shard_map/psum | solution.py:108
  1635.4 1.8 copy.11
  (474 shorter events, 307.0 us)
Async XLA Ops:
  7.2 183.8 %copy-start = (bf16[256,256]{1,0:T(8,128)(2,1)S(1)}, bf16[256,256]{1,0:T(8,128)(2,1)}, u32[]{:S(2)}) copy-start(bf16[256,256]{1,0:T(8,128)(2,1)} %param.16) | copy-start | bytes 393220
  7.2 300.5 %all-gather.3.cloned.1.call-start = ((), (), s32[]{:S(2)}) async-start(), calls=%async_computation.2 | async-start | bytes 2162688 | tf_op jit(solution)/shard_map/all_gather | solution.py:86
  192.6 530.7 %reduce-scatter.3.cloned.1.call-start = ((), (), s32[]{:S(2)}) async-start(), calls=%async_computation.3 | async-start | bytes 4325376 | tf_op jit(solution)/shard_map/reduce_scatter | solution.py:77
  390.1 366.0 %copy-start.2 = (bf16[128,256]{1,0:T(8,128)(2,1)S(1)}, bf16[128,256]{1,0:T(8,128)(2,1)}, u32[]{:S(2)}) copy-start(bf16[128,256]{1,0:T(8,128)(2,1)} %param.21) | copy-start | bytes 196612
  534.7 221.5 %all-reduce.4.cloned.1.call-start = ((), (), s32[]{:S(2)}) async-start(), calls=%async_computation.4 | async-start | bytes 262144 | tf_op jit(solution)/shard_map/psum | solution.py:80
  723.4 108.5 %all-gather.5.cloned.1.call-start = ((), (), s32[]{:S(2)}) async-start(), calls=%async_computation.5 | async-start | bytes 2162688 | tf_op jit(solution)/shard_map/all_gather | solution.py:96
  757.9 491.7 %reduce-scatter.5.cloned.1.call-start = ((), (), s32[]{:S(2)}) async-start(), calls=%async_computation.6 | async-start | bytes 4325376 | tf_op jit(solution)/shard_map/reduce_scatter | solution.py:77
  914.4 368.1 %copy-start.1 = (bf16[128,256]{1,0:T(8,128)(2,1)S(1)}, bf16[128,256]{1,0:T(8,128)(2,1)}, u32[]{:S(2)}) copy-start(bf16[128,256]{1,0:T(8,128)(2,1)} %param.15) | copy-start | bytes 196612
  1059.0 223.6 %all-reduce.6.cloned.1.call-start = ((), (), s32[]{:S(2)}) async-start(), calls=%async_computation.7 | async-start | bytes 262144 | tf_op jit(solution)/shard_map/psum | solution.py:80
  1249.7 385.8 %all-reduce.8.cloned.1.call-start = ((), (), s32[]{:S(2)}) async-start(), calls=%async_computation.8 | async-start | bytes 524288 | tf_op jit(solution)/shard_map/psum | solution.py:108
Sparse Core Ops, SparseCore 0:
  192.7 66.8 all-gather.2
  534.8 188.4 reduce-scatter.2
  725.8 30.3 all-reduce.3
  760.1 71.6 all-gather.4
  1059.1 190.4 reduce-scatter.4
  1252.1 30.3 all-reduce.5
  1285.6 349.7 all-reduce.7
where the time goes:
time: 1670 us; the launch traced here: 1640 us
  waiting for transfers between devices  867 us (52%)
  other arithmetic  231 us (14%)
  matrix products  191 us (11%)
  local copies, waits for them, and re-layouts  145 us (9%)
  loops' own time  126 us (8%)
  blocking collectives  68.3 us (4%)
    reduce_scatter x2, waiting for transfers between devices, collect(): lax.psum_scatter(entity_terms(messages, jnp.int32(0)), 'ent', scatter_dim...  379 us
    psum x1, waiting for transfers between devices, body(): grad_theta = lax.psum(local_theta, 'ent')  349 us
    another operation x2, loops' own time, entity_terms(): pieces = lax.map(block_term, jnp.arange(block_span, dtype=jnp.int32))  125 us
    scatter-add x1, other arithmetic, body(): jax.ops.segment_sum(usable_float.reshape(-1), entity_index.reshape(-1), n...  113 us
    scatter-add x1, other arithmetic, body(): jax.ops.segment_sum(usable_float.reshape(-1), row_lists.reshape(-1), num_...  113 us
    dot_general x64, matrix products, add_block(): jnp.einsum('ps,pf->sf', row_hot, picked, preferred_element_type=jnp.float32)  108 us
    dot_general x64, matrix products, block_term(): jnp.einsum('pw,pf->wf', col_hot, picked, preferred_element_type=jnp.float32)  77.7 us
    all_gather x1, waiting for transfers between devices, body(): lax.all_gather(back_scaled, 'ent', axis=0, tiled=True)  73.9 us
  transfers between devices with their start and end apart: 7, of which 6 were waited for; matrix products, arithmetic and copies ran while one was open for 7% of the time, Pallas kernels for 0%

commit v1 on v0

--- a/solution.py
+++ b/solution.py
@@ -2,6 +2,11 @@
 import jax.numpy as jnp
 from jax import lax
 from jax.sharding import PartitionSpec as P
+
+
+def one_after_other(array, first, second):
+    partial = lax.psum(array, first)
+    return lax.psum(partial, second)
 
 
 def hot_table(indices, live_slots, offset, table_width):
@@ -24,7 +29,7 @@
     local_degree = jax.ops.segment_sum(
         usable_float.reshape(-1), entity_index.reshape(-1), num_segments=blocks_count * ent_dev
     )
-    entity_degree = lax.psum(local_degree, ("ent", "sec"))
+    entity_degree = one_after_other(local_degree, "ent", "sec")
     own_degree = lax.dynamic_slice_in_dim(entity_degree, own_block * ent_dev, ent_dev)
     entity_scale = lax.rsqrt(1.0 + own_degree)[:, None]
     sec_count = jax.ops.segment_sum(

time: 1670 us -> 1790 us (1.072)
  blocking collectives: 68.3 us -> 195 us
    psum x1 -> x2, blocking collectives: 68.3 us -> 195 us  [the longest x1 185 us: one_after_other(): partial = lax.psum(array, first)]
where the time goes in v1:
time: 1790 us; the launch traced here: 1770 us
  waiting for transfers between devices  866 us (48%)
  other arithmetic  231 us (13%)
  blocking collectives  195 us (11%)
  matrix products  191 us (11%)
  local copies, waits for them, and re-layouts  145 us (8%)
  loops' own time  126 us (7%)
    reduce_scatter x2, waiting for transfers between devices, collect(): lax.psum_scatter(entity_terms(messages, jnp.int32(0)), 'ent', scatter_dim...  378 us
    psum x1, waiting for transfers between devices, body(): grad_theta = lax.psum(local_theta, 'ent')  349 us
    psum x1, blocking collectives, one_after_other(): partial = lax.psum(array, first)  185 us
    another operation x2, loops' own time, entity_terms(): pieces = lax.map(block_term, jnp.arange(block_span, dtype=jnp.int32))  125 us
    scatter-add x1, other arithmetic, body(): jax.ops.segment_sum(usable_float.reshape(-1), entity_index.reshape(-1), n...  113 us
    scatter-add x1, other arithmetic, body(): jax.ops.segment_sum(usable_float.reshape(-1), row_lists.reshape(-1), num_...  113 us
    dot_general x64, matrix products, add_block(): jnp.einsum('ps,pf->sf', row_hot, picked, preferred_element_type=jnp.float32)  108 us
    dot_general x64, matrix products, block_term(): jnp.einsum('pw,pf->wf', col_hot, picked, preferred_element_type=jnp.float32)  77.7 us
  transfers between devices with their start and end apart: 7, of which 6 were waited for; matrix products, arithmetic and copies ran while one was open for 7% of the time, Pallas kernels for 0%

profile of v1, /device:TPU:0, one launch (start us, length us, event | category | flops | bytes accessed | tf_op | source)
XLA Modules:
  0.0 1769.7 jit_solution(4529939575746908768)
XLA Ops:
  9.2 113.5 %scatter_custom_fusion = f32[4096]{0:T(1024)S(1)} fusion(s32[16384]{0:T(1024)S(1)} %bitcast.81, f32[16384]{0:T(1024)S(1)} %bitcast.82, f32[]{:T(128)} %constant.131.clone.1), kind=kCustom, calls=%fused_computation.76 | custom fusion | flops 16384 | bytes 16388 | tf_op jit(solution)/shard_map/scatter-add | solution.py:29
  122.6 185.2 %psum.35 = f32[4096]{0:T(1024)S(1)} all-reduce(f32[4096]{0:T(1024)S(1)} %scatter_custom_fusion), channel_id=1, replica_groups=mesh['ent'=32,'sec'=4] {'ent'}, use_global_device_ids=true, to_apply=%region_1.0 | all-reduce | flops 4096 | bytes 32768 | tf_op jit(solution)/shard_map/psum | solution.py:8
  307.8 10.3 psum.36
  320.7 113.4 %scatter_custom_fusion.1 = f32[512]{0:T(512)S(1)} fusion(s32[16384]{0:T(1024)S(1)} %bitcast.84, f32[16384]{0:T(1024)S(1)} %bitcast.83, f32[]{:T(128)} %constant.137.clone.1), kind=kCustom, calls=%fused_computation.78 | custom fusion | flops 16384 | bytes 2052 | tf_op jit(solution)/shard_map/scatter-add | solution.py:35
  434.8 79.9 %while.50 = (s32[]{:T(128)}, f32[512,256]{1,0:T(8,128)S(1)}, s32[32,512]{1,0:T(8,128)}, pred[32,512]{1,0:T(8,128)(4,1)S(1)}, s32[32,512]{1,0:T(8,128)}, /*index=...) while((s32[]{:T(128)}, f32[512,256]{1,0:T(8,128)S(1)}, ...), condition=%wide.region_5.6_spmd.clone, body=%wide.region_4.5_spmd.clone.sunk | while | flops 168820736 | bytes 1128617 | solution.py:60
  445.6 1.7 convolution_add_fusion.4
  448.1 1.7 convolution_add_fusion.4
  463.1 1.7 convolution_add_fusion.4
  465.6 1.7 convolution_add_fusion.4
  480.6 1.7 convolution_add_fusion.4
  483.1 1.7 convolution_add_fusion.4
  498.1 1.7 convolution_add_fusion.4
  500.6 1.7 convolution_add_fusion.4
  514.9 2.4 broadcast.21.clone
  517.3 144.5 %while.48 = (s32[]{:T(128)}, f32[32,128,256]{2,1,0:T(8,128)}, s32[32]{0:T(128)S(1)}, s32[32,512]{1,0:T(8,128)}, pred[32,512]{1,0:T(8,128)(4,1)S(1)}, /*index=5*/...) while((s32[]{:T(128)}, f32[32,128,256]{2,1,0:T(8,128)}, ...), condition=%wide.region_7.8_spmd, body=%wide.region_6.7_spmd.sunk | while | flops 168558592 | bytes 408219 | solution.py:78
  661.9 186.8 %reduce-scatter.3.cloned.1.call-done = f32[128,256]{1,0:T(8,128)} async-done(((f32[4096,256]{1,0:T(8,128)}), f32[128,256]{1,0:T(8,128)}) %reduce-scatter.3.cloned.1.call-update) | async-done | bytes 131088 | tf_op jit(solution)/shard_map/reduce_scatter | solution.py:82
  848.8 32.8 %all-reduce.4.cloned.1.call-done = f32[128,256]{1,0:T(8,128)} async-done(((f32[128,256]{1,0:T(8,128)}), f32[128,256]{1,0:T(8,128)}) %all-reduce.4.cloned.1.call-update) | async-done | bytes 131088 | tf_op jit(solution)/shard_map/psum | solution.py:85
  881.6 1.7 multiply_convert_fusion.3
  883.4 73.9 %all-gather.5.cloned.1.call-done = bf16[4096,256]{1,0:T(8,128)(2,1)} async-done(((bf16[128,256]{1,0:T(8,128)(2,1)}), bf16[4096,256]{1,0:T(8,128)(2,1)}) %all-gather.5.cloned.1.call-update) | async-done | bytes 2097168 | tf_op jit(solution)/shard_map/all_gather | solution.py:101
  957.3 79.9 %while.51 = (s32[]{:T(128)}, f32[512,256]{1,0:T(8,128)S(1)}, s32[32,512]{1,0:T(8,128)}, pred[32,512]{1,0:T(8,128)(4,1)S(1)}, s32[32,512]{1,0:T(8,128)}, /*index=...) while((s32[]{:T(128)}, f32[512,256]{1,0:T(8,128)S(1)}, ...), condition=%wide.region_11.12_spmd.clone, body=%wide.region_10.11_spmd.clone.sunk | while | flops 168820736 | bytes 1128617 | solution.py:60
  970.5 1.7 convolution_add_fusion.5
  973.0 1.7 convolution_add_fusion.5
  988.0 1.7 convolution_add_fusion.5
  990.5 1.7 convolution_add_fusion.5
  1037.4 2.4 broadcast.21
  1039.9 144.5 %while.49 = (s32[]{:T(128)}, f32[32,128,256]{2,1,0:T(8,128)}, s32[32]{0:T(128)S(1)}, s32[32,512]{1,0:T(8,128)}, pred[32,512]{1,0:T(8,128)(4,1)S(1)}, /*index=5*/...) while((s32[]{:T(128)}, f32[32,128,256]{2,1,0:T(8,128)}, ...), condition=%wide.region_13.14_spmd, body=%wide.region_12.13_spmd.sunk | while | flops 168558592 | bytes 408219 | solution.py:78
  1184.4 190.9 %reduce-scatter.5.cloned.1.call-done = f32[128,256]{1,0:T(8,128)} async-done(((f32[4096,256]{1,0:T(8,128)}), f32[128,256]{1,0:T(8,128)}) %reduce-scatter.5.cloned.1.call-update) | async-done | bytes 131088 | tf_op jit(solution)/shard_map/reduce_scatter | solution.py:82
  1375.5 32.7 %all-reduce.6.cloned.1.call-done = f32[128,256]{1,0:T(8,128)} async-done(((f32[128,256]{1,0:T(8,128)}), f32[128,256]{1,0:T(8,128)}) %all-reduce.6.cloned.1.call-update) | async-done | bytes 131088 | tf_op jit(solution)/shard_map/psum | solution.py:85
  1408.2 1.9 convolution_bitcast_fusion
  1410.7 1.7 convolution_convert_fusion.4
  1412.4 348.6 %all-reduce.8.cloned.1.call-done = f32[256,256]{0,1:T(8,128)} async-done(((f32[256,256]{0,1:T(8,128)}), f32[256,256]{0,1:T(8,128)}) %all-reduce.8.cloned.1.call-update) | async-done | bytes 262160 | tf_op jit(solution)/shard_map/psum | solution.py:113
  1761.1 1.8 copy.11
  (475 shorter events, 308.7 us)
Async XLA Ops:
  7.2 311.0 %copy-start = (bf16[256,256]{1,0:T(8,128)(2,1)S(1)}, bf16[256,256]{1,0:T(8,128)(2,1)}, u32[]{:S(2)}) copy-start(bf16[256,256]{1,0:T(8,128)(2,1)} %param.16) | copy-start | bytes 393220
  7.2 427.7 %all-gather.3.cloned.1.call-start = ((), (), s32[]{:S(2)}) async-start(), calls=%async_computation.2 | async-start | bytes 2162688 | tf_op jit(solution)/shard_map/all_gather | solution.py:91
  319.8 529.0 %reduce-scatter.3.cloned.1.call-start = ((), (), s32[]{:S(2)}) async-start(), calls=%async_computation.3 | async-start | bytes 4325376 | tf_op jit(solution)/shard_map/reduce_scatter | solution.py:82
  517.3 364.3 %copy-start.2 = (bf16[128,256]{1,0:T(8,128)(2,1)S(1)}, bf16[128,256]{1,0:T(8,128)(2,1)}, u32[]{:S(2)}) copy-start(bf16[128,256]{1,0:T(8,128)(2,1)} %param.21) | copy-start | bytes 196612
  661.9 219.7 %all-reduce.4.cloned.1.call-start = ((), (), s32[]{:S(2)}) async-start(), calls=%async_computation.4 | async-start | bytes 262144 | tf_op jit(solution)/shard_map/psum | solution.py:85
  848.8 108.5 %all-gather.5.cloned.1.call-start = ((), (), s32[]{:S(2)}) async-start(), calls=%async_computation.5 | async-start | bytes 2162688 | tf_op jit(solution)/shard_map/all_gather | solution.py:101
  883.3 492.1 %reduce-scatter.5.cloned.1.call-start = ((), (), s32[]{:S(2)}) async-start(), calls=%async_computation.6 | async-start | bytes 4325376 | tf_op jit(solution)/shard_map/reduce_scatter | solution.py:82
  1039.8 368.3 %copy-start.1 = (bf16[128,256]{1,0:T(8,128)(2,1)S(1)}, bf16[128,256]{1,0:T(8,128)(2,1)}, u32[]{:S(2)}) copy-start(bf16[128,256]{1,0:T(8,128)(2,1)} %param.15) | copy-start | bytes 196612
  1184.4 223.8 %all-reduce.6.cloned.1.call-start = ((), (), s32[]{:S(2)}) async-start(), calls=%async_computation.7 | async-start | bytes 262144 | tf_op jit(solution)/shard_map/psum | solution.py:85
  1375.4 385.7 %all-reduce.8.cloned.1.call-start = ((), (), s32[]{:S(2)}) async-start(), calls=%async_computation.8 | async-start | bytes 524288 | tf_op jit(solution)/shard_map/psum | solution.py:113
Sparse Core Ops, SparseCore 0:
  319.9 65.0 all-gather.2
  662.0 186.7 reduce-scatter.2
  851.2 30.3 all-reduce.3
  885.5 71.6 all-gather.4
  1184.5 190.8 reduce-scatter.4
  1377.9 30.2 all-reduce.5
  1411.2 349.7 all-reduce.7
